TPU v7x, 32 devices: a whole 2x2x4 slice. The times are simulated.
32 devices in a mesh: dp: 8 (over y, x, core), ctx: 4 (over z).
Axes of the slice: x: 2, y: 2, z: 4, core: 2. Of those that a mesh axis runs over, the one named last changes fastest.
Arguments:
- layer_input: bfloat16 [8, 1024, 1024], P('dp', 'ctx'), may hold values from -6 to 6
- prefix: int32 [8], P('dp'), may hold values from 102 to 512, as said below
- ln1_gain: bfloat16 [1024], P(('dp', 'ctx')), may hold values from 0.5 to 1.5
- ln1_bias: bfloat16 [1024], P(('dp', 'ctx')), may hold values from -3 to 3
- w_qkv: bfloat16 [1024, 3072], P(('dp', 'ctx')), may hold values from -0.1875 to 0.1875
- b_qv: bfloat16 [2048], P(('dp', 'ctx')), may hold values from -4 to 4
- w_out: bfloat16 [1024, 1024], P(('dp', 'ctx')), may hold values from -3 to 3
- b_out: bfloat16 [1024], P(('dp', 'ctx')), may hold values from -3 to 3
- ln2_gain: bfloat16 [1024], P(('dp', 'ctx')), may hold values from 0.5 to 1.5
- ln2_bias: bfloat16 [1024], P(('dp', 'ctx')), may hold values from -3 to 3
- w_up: bfloat16 [1024, 4096], P(('dp', 'ctx')), may hold values from -0.1875 to 0.1875
- b_up: bfloat16 [4096], P(('dp', 'ctx')), may hold values from -4 to 4
- w_down: bfloat16 [4096, 1024], P(('dp', 'ctx')), may hold values from -0.09375 to 0.09375
- b_down: bfloat16 [1024], P(('dp', 'ctx')), may hold values from -6 to 6
- cotangent: bfloat16 [8, 1024, 1024], P('dp', 'ctx'), may hold values from -6 to 6
Outputs:
- layer_out: bfloat16 [8, 1024, 1024], P('dp', 'ctx')
- input_grad: float32 [8, 1024, 1024], P('dp', 'ctx')
- grad_ln1_gain: float32 [1024], P(('dp', 'ctx'))
- grad_ln1_bias: float32 [1024], P(('dp', 'ctx'))
- grad_w_qkv: float32 [1024, 3072], P(('dp', 'ctx'))
- grad_b_qv: float32 [2048], P(('dp', 'ctx'))
- grad_w_out: float32 [1024, 1024], P(('dp', 'ctx'))
- grad_b_out: float32 [1024], P(('dp', 'ctx'))
- grad_ln2_gain: float32 [1024], P(('dp', 'ctx'))
- grad_ln2_bias: float32 [1024], P(('dp', 'ctx'))
- grad_w_up: float32 [1024, 4096], P(('dp', 'ctx'))
- grad_b_up: float32 [4096], P(('dp', 'ctx'))
- grad_w_down: float32 [4096, 1024], P(('dp', 'ctx'))
- grad_b_down: float32 [1024], P(('dp', 'ctx'))
Inputs may be any that keep to these rules, and one draw needn't show every extreme that they name: prefix[s] counts the leading positions of sequence s that attend to one another in both directions; the largest and the smallest allowed values both occur.
All inputs are finite; a program needn't handle non-finite values.
Results may differ from a plain program's by a relative error of at most 0.012.
Values may be sent and summed in bfloat16 or wider, within the bound.
No kernel may reach another device: no remote copies, remote signals or barrier semaphores. Data moves between devices by JAX's collectives and lax.ppermute only.
A program may use at most 192 MiB of HBM per device.

v0:
```python
import jax
import jax.numpy as jnp
from jax import lax
from jax.sharding import PartitionSpec as P

D = 1024
H = 16
HD = 64
NEGATIVE = -1e30


def layer_norm(values, gain, shift):
    center = jnp.mean(values, axis=-1, keepdims=True)
    offsets = values - center
    spread = jnp.mean(offsets * offsets, axis=-1, keepdims=True)
    return offsets * lax.rsqrt(spread + 1e-05) * gain + shift


def gelu_tanh(values):
    return jax.nn.gelu(values, approximate=True)


def masked_scores(query_heads, query_pos, key_heads, key_pos, prefix_len):
    raw_scores = (
        jnp.einsum("qhd,khd->hqk", query_heads, key_heads, preferred_element_type=jnp.float32)
        * 0.125
    )
    allowed = (key_pos[None, :] <= query_pos[:, None]) | (key_pos[None, :] < prefix_len)
    return (jnp.where(allowed[None], raw_scores, NEGATIVE), allowed)


def softmax_rows(query_heads, query_pos, key_heads, key_pos, prefix_len, log_total):
    scores, allowed = masked_scores(query_heads, query_pos, key_heads, key_pos, prefix_len)
    return jnp.where(allowed[None], jnp.exp(scores - log_total[:, :, None]), 0.0)


def per_device(
    layer_input,
    prefix,
    ln1_gain,
    ln1_bias,
    w_qkv,
    b_qv,
    w_out,
    b_out,
    ln2_gain,
    ln2_bias,
    w_up,
    b_up,
    w_down,
    b_down,
    cotangent,
):
    (
        gain_first,
        shift_first,
        proj_qkv,
        bias_qv,
        proj_out,
        bias_out,
        gain_second,
        shift_second,
        proj_up,
        bias_up,
        proj_down,
        bias_down,
    ) = (
        lax.all_gather(ln1_gain, ("dp", "ctx"), axis=0, tiled=True),
        lax.all_gather(ln1_bias, ("dp", "ctx"), axis=0, tiled=True),
        lax.all_gather(w_qkv, ("dp", "ctx"), axis=0, tiled=True),
        lax.all_gather(b_qv, ("dp", "ctx"), axis=0, tiled=True),
        lax.all_gather(w_out, ("dp", "ctx"), axis=0, tiled=True),
        lax.all_gather(b_out, ("dp", "ctx"), axis=0, tiled=True),
        lax.all_gather(ln2_gain, ("dp", "ctx"), axis=0, tiled=True),
        lax.all_gather(ln2_bias, ("dp", "ctx"), axis=0, tiled=True),
        lax.all_gather(w_up, ("dp", "ctx"), axis=0, tiled=True),
        lax.all_gather(b_up, ("dp", "ctx"), axis=0, tiled=True),
        lax.all_gather(w_down, ("dp", "ctx"), axis=0, tiled=True),
        lax.all_gather(b_down, ("dp", "ctx"), axis=0, tiled=True),
    )
    tokens = layer_input.shape[1]
    length = tokens * lax.axis_size("ctx")
    block_rows = min(512, length)
    block_count = length // block_rows
    prefix_len = prefix[0]
    query_pos = lax.axis_index("ctx") * tokens + jnp.arange(tokens, dtype=jnp.int32)
    block_starts = jnp.arange(block_count, dtype=jnp.int32) * block_rows
    local_rows = jnp.arange(block_rows, dtype=jnp.int32)
    inputs = layer_input[0].astype(jnp.float32)
    upstream = cotangent[0].astype(jnp.float32)
    shift_one = shift_first.astype(jnp.float32)
    shift_two = shift_second.astype(jnp.float32)
    hidden_first = layer_norm(inputs, gain_first.astype(jnp.float32), shift_one).astype(
        jnp.bfloat16
    )
    mixed = jnp.dot(hidden_first, proj_qkv, preferred_element_type=jnp.float32)
    bias_pair = bias_qv.astype(jnp.float32)
    queries = (mixed[:, :D] + bias_pair[:D]).astype(jnp.bfloat16)
    keys_own = mixed[:, D : 2 * D].astype(jnp.bfloat16)
    values_own = (mixed[:, 2 * D :] + bias_pair[D:]).astype(jnp.bfloat16)
    keys_all, values_all = (
        lax.all_gather(keys_own, "ctx", axis=0, tiled=True),
        lax.all_gather(values_own, "ctx", axis=0, tiled=True),
    )
    query_heads = queries.reshape(tokens, H, HD)
    key_blocks = keys_all.reshape(block_count, block_rows, H, HD)
    value_blocks = values_all.reshape(block_count, block_rows, H, HD)

    def max_step(state_pair, element):
        key_block, block_start = element
        scores, allowed = masked_scores(
            query_heads, query_pos, key_block, block_start + local_rows, prefix_len
        )
        row_max = jnp.maximum(state_pair[0], jnp.max(scores, axis=-1))
        terms = jnp.where(allowed[None], jnp.exp(scores - row_max[:, :, None]), 0.0)
        row_total = state_pair[1] * jnp.exp(state_pair[0] - row_max) + jnp.sum(terms, axis=-1)
        return ((row_max, row_total), None)

    start_state = (
        jnp.full((H, tokens), NEGATIVE, jnp.float32),
        jnp.zeros((H, tokens), jnp.float32),
    )
    (row_max, row_total), unused = lax.scan(max_step, start_state, (key_blocks, block_starts))
    log_total = row_max + jnp.log(row_total)

    def value_step(attended_sum, element):
        key_block, block_start, value_block = element
        weights_soft = softmax_rows(
            query_heads, query_pos, key_block, block_start + local_rows, prefix_len, log_total
        ).astype(jnp.bfloat16)
        return (
            attended_sum
            + jnp.einsum(
                "hqk,khd->qhd", weights_soft, value_block, preferred_element_type=jnp.float32
            ),
            None,
        )

    attended, unused = lax.scan(
        value_step,
        jnp.zeros((tokens, H, HD), jnp.float32),
        (key_blocks, block_starts, value_blocks),
    )
    attended_low = attended.reshape(tokens, D).astype(jnp.bfloat16)
    branch_one = jnp.dot(
        attended_low, proj_out, preferred_element_type=jnp.float32
    ) + bias_out.astype(jnp.float32)
    resid = inputs + branch_one
    hidden_second = layer_norm(resid, gain_second.astype(jnp.float32), shift_two).astype(
        jnp.bfloat16
    )
    pre_act = jnp.dot(hidden_second, proj_up, preferred_element_type=jnp.float32) + bias_up.astype(
        jnp.float32
    )
    activ = gelu_tanh(pre_act).astype(jnp.bfloat16)
    branch_two = jnp.dot(activ, proj_down, preferred_element_type=jnp.float32) + bias_down.astype(
        jnp.float32
    )
    layer_out = (resid + branch_two).astype(jnp.bfloat16)
    gain_first, proj_qkv, proj_out, gain_second, proj_up, proj_down = (
        lax.all_gather(ln1_gain, ("dp", "ctx"), axis=0, tiled=True),
        lax.all_gather(w_qkv, ("dp", "ctx"), axis=0, tiled=True),
        lax.all_gather(w_out, ("dp", "ctx"), axis=0, tiled=True),
        lax.all_gather(ln2_gain, ("dp", "ctx"), axis=0, tiled=True),
        lax.all_gather(w_up, ("dp", "ctx"), axis=0, tiled=True),
        lax.all_gather(w_down, ("dp", "ctx"), axis=0, tiled=True),
    )
    grad_branch_two = upstream.astype(jnp.bfloat16)
    grad_proj_down = jnp.einsum(
        "tf,td->fd", activ, grad_branch_two, preferred_element_type=jnp.float32
    )
    grad_bias_down = jnp.sum(grad_branch_two.astype(jnp.float32), axis=0)
    grad_activ = jnp.einsum(
        "td,fd->tf", grad_branch_two, proj_down, preferred_element_type=jnp.float32
    )
    gelu_value, gelu_pull = jax.vjp(gelu_tanh, pre_act)
    grad_pre = gelu_pull(grad_activ)[0].astype(jnp.bfloat16)
    grad_proj_up = jnp.einsum(
        "td,tf->df", hidden_second, grad_pre, preferred_element_type=jnp.float32
    )
    grad_bias_up = jnp.sum(grad_pre.astype(jnp.float32), axis=0)
    grad_hidden_second = jnp.einsum(
        "tf,df->td", grad_pre, proj_up, preferred_element_type=jnp.float32
    )
    norm_value, norm_pull = jax.vjp(layer_norm, resid, gain_second.astype(jnp.float32), shift_two)
    resid_part, grad_gain_second, grad_shift_second = norm_pull(grad_hidden_second)
    grad_resid = upstream + resid_part
    grad_branch_one = grad_resid.astype(jnp.bfloat16)
    grad_proj_out = jnp.einsum(
        "td,te->de", attended_low, grad_branch_one, preferred_element_type=jnp.float32
    )
    grad_bias_out = jnp.sum(grad_branch_one.astype(jnp.float32), axis=0)
    grad_attended = jnp.einsum(
        "te,de->td", grad_branch_one, proj_out, preferred_element_type=jnp.float32
    ).astype(jnp.bfloat16)
    grad_heads = grad_attended.reshape(tokens, H, HD)
    row_delta = jnp.sum(grad_heads.astype(jnp.float32) * attended, axis=-1).T

    def back_step(query_sum, element):
        key_block, block_start, value_block = element
        weights_soft = softmax_rows(
            query_heads, query_pos, key_block, block_start + local_rows, prefix_len, log_total
        )
        value_grad = jnp.einsum(
            "hqk,qhd->khd",
            weights_soft.astype(jnp.bfloat16),
            grad_heads,
            preferred_element_type=jnp.float32,
        )
        weight_grad = jnp.einsum(
            "qhd,khd->hqk", grad_heads, value_block, preferred_element_type=jnp.float32
        )
        score_grad = (weights_soft * (weight_grad - row_delta[:, :, None])).astype(jnp.bfloat16)
        query_sum = (
            query_sum
            + jnp.einsum("hqk,khd->qhd", score_grad, key_block, preferred_element_type=jnp.float32)
            * 0.125
        )
        key_grad = (
            jnp.einsum("hqk,qhd->khd", score_grad, query_heads, preferred_element_type=jnp.float32)
            * 0.125
        )
        return (query_sum, (key_grad.reshape(block_rows, D), value_grad.reshape(block_rows, D)))

    query_sum, (key_terms, value_terms) = lax.scan(
        back_step, jnp.zeros((tokens, H, HD), jnp.float32), (key_blocks, block_starts, value_blocks)
    )
    key_sum, value_sum = (
        lax.psum_scatter(
            key_terms.reshape(length, D).astype(jnp.bfloat16),
            "ctx",
            scatter_dimension=0,
            tiled=True,
        ).astype(jnp.float32),
        lax.psum_scatter(
            value_terms.reshape(length, D).astype(jnp.bfloat16),
            "ctx",
            scatter_dimension=0,
            tiled=True,
        ).astype(jnp.float32),
    )
    query_low = query_sum.reshape(tokens, D).astype(jnp.bfloat16)
    key_low = key_sum.astype(jnp.bfloat16)
    value_low = value_sum.astype(jnp.bfloat16)
    grad_qkv = jnp.concatenate([query_low, key_low, value_low], axis=1)
    grad_proj_qkv = jnp.einsum(
        "td,te->de", hidden_first, grad_qkv, preferred_element_type=jnp.float32
    )
    grad_bias_qv = jnp.concatenate(
        [
            jnp.sum(query_low.astype(jnp.float32), axis=0),
            jnp.sum(value_low.astype(jnp.float32), axis=0),
        ]
    )
    grad_hidden_first = jnp.einsum(
        "te,de->td", grad_qkv, proj_qkv, preferred_element_type=jnp.float32
    )
    first_value, first_pull = jax.vjp(layer_norm, inputs, gain_first.astype(jnp.float32), shift_one)
    input_part, grad_gain_first, grad_shift_first = first_pull(grad_hidden_first)
    input_grad = grad_resid + input_part
    (
        sum_gain_first,
        sum_shift_first,
        sum_qkv,
        sum_bias_qv,
        sum_out,
        sum_bias_out,
        sum_gain_second,
        sum_shift_second,
        sum_up,
        sum_bias_up,
        sum_down,
        sum_bias_down,
    ) = (
        lax.psum_scatter(grad_gain_first, ("dp", "ctx"), scatter_dimension=0, tiled=True),
        lax.psum_scatter(grad_shift_first, ("dp", "ctx"), scatter_dimension=0, tiled=True),
        lax.psum_scatter(grad_proj_qkv, ("dp", "ctx"), scatter_dimension=0, tiled=True),
        lax.psum_scatter(grad_bias_qv, ("dp", "ctx"), scatter_dimension=0, tiled=True),
        lax.psum_scatter(grad_proj_out, ("dp", "ctx"), scatter_dimension=0, tiled=True),
        lax.psum_scatter(grad_bias_out, ("dp", "ctx"), scatter_dimension=0, tiled=True),
        lax.psum_scatter(grad_gain_second, ("dp", "ctx"), scatter_dimension=0, tiled=True),
        lax.psum_scatter(grad_shift_second, ("dp", "ctx"), scatter_dimension=0, tiled=True),
        lax.psum_scatter(grad_proj_up, ("dp", "ctx"), scatter_dimension=0, tiled=True),
        lax.psum_scatter(grad_bias_up, ("dp", "ctx"), scatter_dimension=0, tiled=True),
        lax.psum_scatter(grad_proj_down, ("dp", "ctx"), scatter_dimension=0, tiled=True),
        lax.psum_scatter(grad_bias_down, ("dp", "ctx"), scatter_dimension=0, tiled=True),
    )
    return (
        layer_out[None],
        input_grad[None],
        sum_gain_first,
        sum_shift_first,
        sum_qkv,
        sum_bias_qv,
        sum_out,
        sum_bias_out,
        sum_gain_second,
        sum_shift_second,
        sum_up,
        sum_bias_up,
        sum_down,
        sum_bias_down,
    )


def solution(mesh):
    placed = (
        P("dp", "ctx", None),
        P("dp"),
        P(("dp", "ctx")),
        P(("dp", "ctx")),
        P(("dp", "ctx"), None),
        P(("dp", "ctx")),
        P(("dp", "ctx"), None),
        P(("dp", "ctx")),
        P(("dp", "ctx")),
        P(("dp", "ctx")),
        P(("dp", "ctx"), None),
        P(("dp", "ctx")),
        P(("dp", "ctx"), None),
        P(("dp", "ctx")),
        P("dp", "ctx", None),
    )
    return jax.shard_map(
        per_device,
        mesh=mesh,
        in_specs=placed,
        out_specs=(
            P("dp", "ctx", None),
            P("dp", "ctx", None),
            P(("dp", "ctx")),
            P(("dp", "ctx")),
            P(("dp", "ctx"), None),
            P(("dp", "ctx")),
            P(("dp", "ctx"), None),
            P(("dp", "ctx")),
            P(("dp", "ctx")),
            P(("dp", "ctx")),
            P(("dp", "ctx"), None),
            P(("dp", "ctx")),
            P(("dp", "ctx"), None),
            P(("dp", "ctx")),
        ),
        check_vma=False,
    )
```

profile of v0, /device:TPU:0, one launch (start us, length us, event | category | flops | bytes accessed | tf_op | source)
XLA Modules:
  0.0 1624.3 jit_solution(12898448946622320328)
XLA Ops:
  13.8 42.5 %all-reduce.16 = (bf16[1024]{0:T(1024)(128)(2,1)S(1)}, bf16[1024]{0:T(1024)(128)(2,1)S(1)}, bf16[2048]{0:T(1024)(128)(2,1)S(1)}, bf16[1024]{0:T(1024)(128)(2,1)S...) all-reduce(bf16[1024]{0:T(1024)(128)(2,1)S(1)} %dynamic-update-slic, ...), channel_id=1, replica_groups=mesh['dp'=8,'ctx'=4] {'dp','ctx'}, use_global_device_ids=true, to_apply=%add.1 | all-reduce | flops 8192 | bytes 32768
  59.5 23.9 %all-gather.8.cloned.1.call-done = bf16[1024,3072]{1,0:T(8,128)(2,1)} async-done(((bf16[32,3072]{1,0:T(8,128)(2,1)}), bf16[1024,3072]{1,0:T(8,128)(2,1)}) %all-gather.8.cloned.1.call-update) | async-done | bytes 6291472 | tf_op jit(solution)/shard_map/all_gather | solution.py:70
  92.4 66.4 %all-gather = bf16[32,1,128]{2,1,0:T(2,128)(2,1)S(1)} all-gather(bf16[1,1,128]{2,1,0:T(2,128)(2,1)S(1)} %bitcast.227), channel_id=1, replica_groups=mesh['dp'=8,'ctx'=4] {'dp','ctx'}, dimensions={0}, use_global_device_ids=true | all-gather | bytes 8448 | tf_op jit(solution)/shard_map/all_gather | solution.py:77
  172.0 9.4 all-gather.12.cloned.1.call-done
  192.3 24.0 %while.39 = (s32[]{:T(128)}, f32[16,256]{1,0:T(8,128)S(1)}, f32[16,256]{1,0:T(8,128)S(1)}, s32[2]{0:T(128)S(1)}, s32[]{:T(128)}, /*index=5*/bf16[2,512,16,64]{1,...) while((s32[]{:T(128)}, f32[16,256]{1,0:T(8,128)S(1)}, ...), condition=%wide.region_5.6_spmd.clone, body=%wide.region_2.5_spmd.clone.sunk | while | flops 285497088 | bytes 18963608 | solution.py:123
  216.3 16.0 while.40
  243.3 75.1 %all-gather.16.cloned.1.call-done = bf16[1024,4096]{1,0:T(8,128)(2,1)} async-done(((bf16[32,4096]{1,0:T(8,128)(2,1)}), bf16[1024,4096]{1,0:T(8,128)(2,1)}) %all-gather.16.cloned.1.call-update) | async-done | bytes 8388624 | tf_op jit(solution)/shard_map/all_gather | solution.py:76
  318.5 8.2 convolution_add_fusion
  326.7 70.6 %all-gather.18.cloned.1.call-done = bf16[4096,1024]{1,0:T(8,128)(2,1)} async-done(((bf16[128,1024]{1,0:T(8,128)(2,1)}), bf16[4096,1024]{1,0:T(8,128)(2,1)}) %all-gather.18.cloned.1.call-update) | async-done | bytes 8388624 | tf_op jit(solution)/shard_map/all_gather | solution.py:78
  397.3 8.7 convert_reduce_fusion
  418.6 63.5 %while.41 = (s32[]{:T(128)}, f32[256,16,64]{0,2,1:T(8,128)}, bf16[2,512,1024]{2,1,0:T(8,128)(2,1)}, bf16[2,512,1024]{2,1,0:T(8,128)(2,1)}, bf16[2,512,16,64]{1,3...) while((s32[]{:T(128)}, f32[256,16,64]{0,2,1:T(8,128)}, ...), condition=%wide.region_14.15_spmd.clone, body=%wide.region_13.14_spmd.clone.sunk | while | flops 1369442048 | bytes 102161728 | solution.py:225
  431.5 6.5 fusion.181
  463.3 6.5 fusion.181
  494.0 34.7 %reduce-scatter.9.cloned.1.call-done = bf16[256,1024]{0,1:T(8,128)(2,1)} async-done(((bf16[1024,1024]{0,1:T(8,128)(2,1)}), bf16[256,1024]{0,1:T(8,128)(2,1)}) %reduce-scatter.9.cloned.1.call-update) | async-done | bytes 524304 | tf_op jit(solution)/shard_map/reduce_scatter | solution.py:235
  528.8 45.6 %reduce-scatter.7.cloned.1.call-done = bf16[256,1024]{0,1:T(8,128)(2,1)} async-done(((bf16[1024,1024]{0,1:T(8,128)(2,1)}), bf16[256,1024]{0,1:T(8,128)(2,1)}) %reduce-scatter.7.cloned.1.call-update) | async-done | bytes 524304 | tf_op jit(solution)/shard_map/reduce_scatter | solution.py:229
  574.4 7.7 fusion.93
  583.4 9.8 fusion.109
  594.3 10.7 fusion.95
  605.7 8.3 fusion.82
  621.4 41.1 %all-reduce.15 = (f32[1024]{0:T(1024)S(1)}, f32[1024]{0:T(1024)S(1)}, f32[2048]{0:T(1024)S(1)}, f32[1024]{0:T(1024)S(1)}, f32[1024]{0:T(1024)S(1)}, /*index=5*/f...) all-reduce(f32[1024]{0:T(1024)S(1)} %get-tuple-element.430, ...), channel_id=4, replica_groups=mesh['dp'=8,'ctx'=4] {'dp','ctx'}, use_global_device_ids=true, to_apply=%region_20.21.clone | all-reduce | flops 12288 | bytes 98304
  667.1 58.2 %reduce-scatter.13.cloned.1.call-done = f32[32,1024]{1,0:T(8,128)} async-done(((f32[1024,1024]{1,0:T(8,128)}), f32[32,1024]{1,0:T(8,128)}) %reduce-scatter.13.cloned.1.call-update) | async-done | bytes 131088 | tf_op jit(solution)/shard_map/reduce_scatter | solution.py:279
  725.3 160.5 %reduce-scatter.11.cloned.1.call-done = f32[32,3072]{1,0:T(8,128)} async-done(((f32[1024,3072]{1,0:T(8,128)}), f32[32,3072]{1,0:T(8,128)}) %reduce-scatter.11.cloned.1.call-update) | async-done | bytes 393232 | tf_op jit(solution)/shard_map/reduce_scatter | solution.py:277
  885.8 366.4 %reduce-scatter.15.cloned.1.call-done = f32[32,4096]{1,0:T(8,128)} async-done(((f32[1024,4096]{1,0:T(8,128)}), f32[32,4096]{1,0:T(8,128)}) %reduce-scatter.15.cloned.1.call-update) | async-done | bytes 524304 | tf_op jit(solution)/shard_map/reduce_scatter | solution.py:283
  1252.2 365.0 %reduce-scatter.17.cloned.1.call-done = f32[128,1024]{1,0:T(8,128)} async-done(((f32[4096,1024]{1,0:T(8,128)}), f32[128,1024]{1,0:T(8,128)}) %reduce-scatter.17.cloned.1.call-update) | async-done | bytes 524304 | tf_op jit(solution)/shard_map/reduce_scatter | solution.py:285
  (247 shorter events, 183.0 us)
Async XLA Ops:
  7.2 76.2 %all-gather.8.cloned.1.call-start = ((), (), s32[]{:S(2)}) async-start(), calls=%async_computation.6 | async-start | bytes 6488064 | tf_op jit(solution)/shard_map/all_gather | solution.py:70
  7.9 152.2 %all-gather.10.cloned.1.call-start = ((), (), s32[]{:S(2)}) async-start(), calls=%async_computation.7 | async-start | bytes 2621440 | tf_op jit(solution)/shard_map/all_gather | solution.py:103
  56.4 31.9 %copy-start.24 = (f32[1024]{0:T(1024)}, f32[1024]{0:T(1024)S(1)}, u32[]{:S(2)}) copy-start(f32[1024]{0:T(1024)S(1)} %convert_element_type.122) | copy-start | bytes 12292
  56.4 31.9 %copy-start.22 = (f32[1024]{0:T(1024)}, f32[1024]{0:T(1024)S(1)}, u32[]{:S(2)}) copy-start(f32[1024]{0:T(1024)S(1)} %convert_element_type.121) | copy-start | bytes 12292
  57.6 30.7 %copy-start.26 = (f32[256]{0:T(256)}, f32[256]{0:T(256)S(1)}, u32[]{:S(2)}) copy-start(f32[256]{0:T(256)S(1)} %broadcast_multiply_fusion.1) | copy-start | bytes 3076
  58.9 29.3 %copy-start.28 = (f32[256]{0:T(256)}, f32[256]{0:T(256)S(1)}, u32[]{:S(2)}) copy-start(f32[256]{0:T(256)S(1)} %fusion.101) | copy-start | bytes 3076
  89.5 91.8 %all-gather.12.cloned.1.call-start = ((), (), s32[]{:S(2)}) async-start(), calls=%async_computation.8 | async-start | bytes 2621440 | tf_op jit(solution)/shard_map/all_gather | solution.py:102
  90.5 148.9 %all-gather.14.cloned.1.call-start = ((), (), s32[]{:S(2)}) async-start(), calls=%async_computation.9 | async-start | bytes 2162688 | tf_op jit(solution)/shard_map/all_gather | solution.py:72
  91.1 227.4 %all-gather.16.cloned.1.call-start = ((), (), s32[]{:S(2)}) async-start(), calls=%async_computation.10 | async-start | bytes 8650752 | tf_op jit(solution)/shard_map/all_gather | solution.py:76
  91.7 305.6 %all-gather.18.cloned.1.call-start = ((), (), s32[]{:S(2)}) async-start(), calls=%async_computation.11 | async-start | bytes 8650752 | tf_op jit(solution)/shard_map/all_gather | solution.py:78
  92.2 436.5 %reduce-scatter.9.cloned.1.call-start = ((), (), s32[]{:S(2)}) async-start(), calls=%async_computation.13 | async-start | bytes 2621440 | tf_op jit(solution)/shard_map/reduce_scatter | solution.py:235
  216.3 23.1 %copy-start.2 = (bf16[1,256,1024]{2,1,0:T(8,128)(2,1)S(1)}, bf16[1,256,1024]{2,1,0:T(8,128)(2,1)}, u32[]{:S(2)}) copy-start(bf16[1,256,1024]{2,1,0:T(8,128)(2,1)} %param.21) | copy-start | bytes 1572868
  397.3 10.0 copy-start.4
  397.3 10.0 copy-start.40
  486.1 88.2 %reduce-scatter.7.cloned.1.call-start = ((), (), s32[]{:S(2)}) async-start(), calls=%async_computation.12 | async-start | bytes 2621440 | tf_op jit(solution)/shard_map/reduce_scatter | solution.py:229
  488.8 236.5 %reduce-scatter.13.cloned.1.call-start = ((), (), s32[]{:S(2)}) async-start(), calls=%async_computation.15 | async-start | bytes 4325376 | tf_op jit(solution)/shard_map/reduce_scatter | solution.py:279
  492.6 81.8 %copy-start.23 = (f32[1024]{0:T(1024)S(1)}, f32[1024]{0:T(1024)}, u32[]{:S(2)}) copy-start(f32[1024]{0:T(1024)} %copy-done.22) | copy-start | bytes 12292
  492.6 81.8 %copy-start.25 = (f32[1024]{0:T(1024)S(1)}, f32[1024]{0:T(1024)}, u32[]{:S(2)}) copy-start(f32[1024]{0:T(1024)} %copy-done.24) | copy-start | bytes 12292
  492.6 81.8 %copy-start.27 = (f32[256]{0:T(256)S(1)}, f32[256]{0:T(256)}, u32[]{:S(2)}) copy-start(f32[256]{0:T(256)} %copy-done.26) | copy-start | bytes 3076
  492.6 81.8 %copy-start.29 = (f32[256]{0:T(256)S(1)}, f32[256]{0:T(256)}, u32[]{:S(2)}) copy-start(f32[256]{0:T(256)} %copy-done.28) | copy-start | bytes 3076
  492.6 393.2 %reduce-scatter.11.cloned.1.call-start = ((), (), s32[]{:S(2)}) async-start(), calls=%async_computation.14 | async-start | bytes 12976128 | tf_op jit(solution)/shard_map/reduce_scatter | solution.py:277
  494.0 88.1 %copy-start.12 = (bf16[256,16,64]{0,2,1:T(8,128)(2,1)}, bf16[256,16,64]{0,2,1:T(8,128)(2,1)S(1)}, u32[]{:S(2)}) copy-start(bf16[256,16,64]{0,2,1:T(8,128)(2,1)S(1)} %get-tuple-element.513) | copy-start | bytes 1572868
  582.2 670.0 %reduce-scatter.15.cloned.1.call-start = ((), (), s32[]{:S(2)}) async-start(), calls=%async_computation.16 | async-start | bytes 17301504 | tf_op jit(solution)/shard_map/reduce_scatter | solution.py:283
  593.2 1024.0 %reduce-scatter.17.cloned.1.call-start = ((), (), s32[]{:S(2)}) async-start(), calls=%async_computation.17 | async-start | bytes 17301504 | tf_op jit(solution)/shard_map/reduce_scatter | solution.py:285
  (33 other events, 122.4 us)
Sparse Core Ops, SparseCore 0:
  10.9 72.4 all-gather.7
  89.7 44.5 all-gather.9
  136.4 44.8 all-gather.11
  184.2 55.2 all-gather.13
  242.2 76.2 all-gather.15
  321.2 75.9 all-gather.17
  486.3 42.4 reduce-scatter.8
  531.1 43.1 reduce-scatter.6
  577.2 148.0 reduce-scatter.12
  731.8 153.9 reduce-scatter.10
  888.8 363.3 reduce-scatter.14
  1255.0 362.1 reduce-scatter.16
where the time goes:
time: 1630 us; the launch traced here: 1620 us
  waiting for transfers between devices  1220 us (75%)
  blocking collectives  150 us (9%)
  matrix products  136 us (8%)
  local copies, waits for them, and re-layouts  71.7 us (4%)
  other arithmetic  33.5 us (2%)
    reduce_scatter x1, waiting for transfers between devices, per_device(): lax.psum_scatter(grad_proj_up, ('dp', 'ctx'), scatter_dimension=0, tiled=...  366 us
    reduce_scatter x1, waiting for transfers between devices, per_device(): lax.psum_scatter(grad_proj_down, ('dp', 'ctx'), scatter_dimension=0, tile...  365 us
    reduce_scatter x1, waiting for transfers between devices, per_device(): lax.psum_scatter(grad_proj_qkv, ('dp', 'ctx'), scatter_dimension=0, tiled...  160 us
    unnamed x2, blocking collectives  83.6 us
    all_gather x1, waiting for transfers between devices, per_device(): lax.all_gather(w_up, ('dp', 'ctx'), axis=0, tiled=True)  75.1 us
    all_gather x1, waiting for transfers between devices, per_device(): lax.all_gather(w_down, ('dp', 'ctx'), axis=0, tiled=True)  70.6 us
    all_gather x1, blocking collectives, per_device(): lax.all_gather(b_up, ('dp', 'ctx'), axis=0, tiled=True)  66.4 us
    reduce_scatter x1, waiting for transfers between devices, per_device(): lax.psum_scatter(grad_proj_out, ('dp', 'ctx'), scatter_dimension=0, tiled...  58.2 us
  transfers between devices with their start and end apart: 12, of which 11 were waited for; matrix products, arithmetic and copies ran while one was open for 9% of the time, Pallas kernels for 0%

commit v1 on v0

--- a/solution.py
+++ b/solution.py
@@ -7,6 +7,29 @@
 H = 16
 HD = 64
 NEGATIVE = -1e30
+
+
+def in_order(parts, dim):
+    parts = jnp.moveaxis(parts, 0, dim)
+    dims = parts.shape
+    return parts.reshape(*dims[:dim], dims[dim] * dims[dim + 1], *dims[dim + 2 :])
+
+
+def doubled(shard, axis):
+    size, index = (lax.axis_size(axis), lax.axis_index(axis))
+    tiles, bit = (shard[None], 1)
+    while bit < size:
+        partner_block = lax.ppermute(tiles, axis, [(i, i ^ bit) for i in range(size)])
+        low = index & bit == 0
+        tiles = jnp.concatenate(
+            [jnp.where(low, tiles, partner_block), jnp.where(low, partner_block, tiles)]
+        )
+        bit *= 2
+    return tiles
+
+
+def doubled_up(x, axis, dim):
+    return in_order(doubled(x, axis), dim)
 
 
 def layer_norm(values, gain, shift):
@@ -74,7 +97,7 @@
         lax.all_gather(ln2_gain, ("dp", "ctx"), axis=0, tiled=True),
         lax.all_gather(ln2_bias, ("dp", "ctx"), axis=0, tiled=True),
         lax.all_gather(w_up, ("dp", "ctx"), axis=0, tiled=True),
-        lax.all_gather(b_up, ("dp", "ctx"), axis=0, tiled=True),
+        doubled_up(b_up, ("dp", "ctx"), 0),
         lax.all_gather(w_down, ("dp", "ctx"), axis=0, tiled=True),
         lax.all_gather(b_down, ("dp", "ctx"), axis=0, tiled=True),
     )

time: 1630 us -> 1630 us (level)
  blocking collectives: 150 us -> 83.5 us
  waiting for transfers between devices: 1220 us -> 1270 us
    all_gather x1 -> x0, blocking collectives: 66.4 us -> none  [per_device(): lax.all_gather(b_up, ('dp', 'ctx'), axis=0, tiled=True)]
    all_gather x1, waiting for transfers between devices: 9.36 us -> 34.4 us  [per_device(): lax.all_gather(keys_own, 'ctx', axis=0, tiled=True)]
    all_gather x1, waiting for transfers between devices: 0.02 us -> 23.8 us  [per_device(): lax.all_gather(values_own, 'ctx', axis=0, tiled=True)]
  transfers between devices with their start and end apart: 12 -> 17, of which waited for: 11 -> 17; matrix products, arithmetic and copies ran while one was open for 9% -> 9% of each run, Pallas kernels for 0% -> 0%
where the time goes in v1:
time: 1630 us; the launch traced here: 1620 us
  waiting for transfers between devices  1270 us (78%)
  matrix products  136 us (8%)
  blocking collectives  83.5 us (5%)
  local copies, waits for them, and re-layouts  72.3 us (4%)
  other arithmetic  33.6 us (2%)
    reduce_scatter x1, waiting for transfers between devices, per_device(): lax.psum_scatter(grad_proj_up, ('dp', 'ctx'), scatter_dimension=0, tiled=...  366 us
    reduce_scatter x1, waiting for transfers between devices, per_device(): lax.psum_scatter(grad_proj_down, ('dp', 'ctx'), scatter_dimension=0, tile...  365 us
    reduce_scatter x1, waiting for transfers between devices, per_device(): lax.psum_scatter(grad_proj_qkv, ('dp', 'ctx'), scatter_dimension=0, tiled...  160 us
    unnamed x2, blocking collectives  83.5 us
    all_gather x1, waiting for transfers between devices, per_device(): lax.all_gather(w_up, ('dp', 'ctx'), axis=0, tiled=True)  75.2 us
    all_gather x1, waiting for transfers between devices, per_device(): lax.all_gather(w_down, ('dp', 'ctx'), axis=0, tiled=True)  70.6 us
    reduce_scatter x1, waiting for transfers between devices, per_device(): lax.psum_scatter(grad_proj_out, ('dp', 'ctx'), scatter_dimension=0, tiled...  58.2 us
    reduce_scatter x1, waiting for transfers between devices, per_device(): lax.psum_scatter(key_terms.reshape(length, D).astype(jnp.bfloat16), 'ctx'...  45.6 us
  transfers between devices with their start and end apart: 17, of which 17 were waited for; matrix products, arithmetic and copies ran while one was open for 9% of the time, Pallas kernels for 0%

profile of v1, /device:TPU:0, one launch (start us, length us, event | category | flops | bytes accessed | tf_op | source)
XLA Modules:
  0.0 1623.2 jit_solution(14842329164817118260)
XLA Ops:
  13.8 42.5 %all-reduce.16 = (bf16[1024]{0:T(1024)(128)(2,1)S(1)}, bf16[1024]{0:T(1024)(128)(2,1)S(1)}, bf16[2048]{0:T(1024)(128)(2,1)S(1)}, bf16[1024]{0:T(1024)(128)(2,1)S...) all-reduce(bf16[1024]{0:T(1024)(128)(2,1)S(1)} %dynamic-update-slic, ...), channel_id=1, replica_groups=mesh['dp'=8,'ctx'=4] {'dp','ctx'}, use_global_device_ids=true, to_apply=%add.1 | all-reduce | flops 8192 | bytes 32768
  59.5 23.9 %all-gather.7.cloned.1.call-done = bf16[1024,3072]{1,0:T(8,128)(2,1)} async-done(((bf16[32,3072]{1,0:T(8,128)(2,1)}), bf16[1024,3072]{1,0:T(8,128)(2,1)}) %all-gather.7.cloned.1.call-update) | async-done | bytes 6291472 | tf_op jit(solution)/shard_map/all_gather | solution.py:93
  110.4 23.8 %all-gather.9.cloned.1.call-done = bf16[1024,1024]{1,0:T(8,128)(2,1)} async-done(((bf16[256,1024]{1,0:T(8,128)(2,1)}), bf16[1024,1024]{1,0:T(8,128)(2,1)}) %all-gather.9.cloned.1.call-update) | async-done | bytes 2097168 | tf_op jit(solution)/shard_map/all_gather | solution.py:126
  134.2 6.9 reshape.297
  146.6 34.4 %all-gather.11.cloned.1.call-done = bf16[1024,1024]{1,0:T(8,128)(2,1)} async-done(((bf16[256,1024]{1,0:T(8,128)(2,1)}), bf16[1024,1024]{1,0:T(8,128)(2,1)}) %all-gather.11.cloned.1.call-update) | async-done | bytes 2097168 | tf_op jit(solution)/shard_map/all_gather | solution.py:125
  191.9 24.0 %while.39 = (s32[]{:T(128)}, f32[16,256]{1,0:T(8,128)S(1)}, f32[16,256]{1,0:T(8,128)S(1)}, s32[2]{0:T(128)S(1)}, s32[]{:T(128)}, /*index=5*/bf16[2,512,16,64]{1,...) while((s32[]{:T(128)}, f32[16,256]{1,0:T(8,128)S(1)}, ...), condition=%wide.region_5.6_spmd.clone, body=%wide.region_2.5_spmd.clone.sunk | while | flops 285497088 | bytes 18963608 | solution.py:146
  216.0 16.0 while.40
  242.9 75.2 %all-gather.15.cloned.1.call-done = bf16[1024,4096]{1,0:T(8,128)(2,1)} async-done(((bf16[32,4096]{1,0:T(8,128)(2,1)}), bf16[1024,4096]{1,0:T(8,128)(2,1)}) %all-gather.15.cloned.1.call-update) | async-done | bytes 8388624 | tf_op jit(solution)/shard_map/all_gather | solution.py:99
  318.1 8.2 convolution_add_fusion
  326.3 70.6 %all-gather.17.cloned.1.call-done = bf16[4096,1024]{1,0:T(8,128)(2,1)} async-done(((bf16[128,1024]{1,0:T(8,128)(2,1)}), bf16[4096,1024]{1,0:T(8,128)(2,1)}) %all-gather.17.cloned.1.call-update) | async-done | bytes 8388624 | tf_op jit(solution)/shard_map/all_gather | solution.py:101
  396.9 8.7 convert_reduce_fusion
  418.2 63.5 %while.41 = (s32[]{:T(128)}, f32[256,16,64]{0,2,1:T(8,128)}, bf16[2,512,1024]{2,1,0:T(8,128)(2,1)}, bf16[2,512,1024]{2,1,0:T(8,128)(2,1)}, bf16[2,512,16,64]{1,3...) while((s32[]{:T(128)}, f32[256,16,64]{0,2,1:T(8,128)}, ...), condition=%wide.region_14.15_spmd.clone, body=%wide.region_13.14_spmd.clone.sunk | while | flops 1369442048 | bytes 102161728 | solution.py:248
  462.9 6.5 fusion.182
  493.7 34.7 %reduce-scatter.9.cloned.1.call-done = bf16[256,1024]{0,1:T(8,128)(2,1)} async-done(((bf16[1024,1024]{0,1:T(8,128)(2,1)}), bf16[256,1024]{0,1:T(8,128)(2,1)}) %reduce-scatter.9.cloned.1.call-update) | async-done | bytes 524304 | tf_op jit(solution)/shard_map/reduce_scatter | solution.py:258
  528.4 45.6 %reduce-scatter.7.cloned.1.call-done = bf16[256,1024]{0,1:T(8,128)(2,1)} async-done(((bf16[1024,1024]{0,1:T(8,128)(2,1)}), bf16[256,1024]{0,1:T(8,128)(2,1)}) %reduce-scatter.7.cloned.1.call-update) | async-done | bytes 524304 | tf_op jit(solution)/shard_map/reduce_scatter | solution.py:252
  574.0 7.7 fusion.93
  583.0 9.8 fusion.110
  593.8 10.7 fusion.95
  605.3 8.3 fusion.82
  621.0 41.0 %all-reduce.15 = (f32[1024]{0:T(1024)S(1)}, f32[1024]{0:T(1024)S(1)}, f32[2048]{0:T(1024)S(1)}, f32[1024]{0:T(1024)S(1)}, f32[1024]{0:T(1024)S(1)}, /*index=5*/f...) all-reduce(f32[1024]{0:T(1024)S(1)} %get-tuple-element.430, ...), channel_id=4, replica_groups=mesh['dp'=8,'ctx'=4] {'dp','ctx'}, use_global_device_ids=true, to_apply=%region_20.21.clone | all-reduce | flops 12288 | bytes 98304
  666.7 58.2 %reduce-scatter.13.cloned.1.call-done = f32[32,1024]{1,0:T(8,128)} async-done(((f32[1024,1024]{1,0:T(8,128)}), f32[32,1024]{1,0:T(8,128)}) %reduce-scatter.13.cloned.1.call-update) | async-done | bytes 131088 | tf_op jit(solution)/shard_map/reduce_scatter | solution.py:302
  724.9 159.9 %reduce-scatter.11.cloned.1.call-done = f32[32,3072]{1,0:T(8,128)} async-done(((f32[1024,3072]{1,0:T(8,128)}), f32[32,3072]{1,0:T(8,128)}) %reduce-scatter.11.cloned.1.call-update) | async-done | bytes 393232 | tf_op jit(solution)/shard_map/reduce_scatter | solution.py:300
  884.8 366.3 %reduce-scatter.15.cloned.1.call-done = f32[32,4096]{1,0:T(8,128)} async-done(((f32[1024,4096]{1,0:T(8,128)}), f32[32,4096]{1,0:T(8,128)}) %reduce-scatter.15.cloned.1.call-update) | async-done | bytes 524304 | tf_op jit(solution)/shard_map/reduce_scatter | solution.py:306
  1251.1 365.0 %reduce-scatter.17.cloned.1.call-done = f32[128,1024]{1,0:T(8,128)} async-done(((f32[4096,1024]{1,0:T(8,128)}), f32[128,1024]{1,0:T(8,128)}) %reduce-scatter.17.cloned.1.call-update) | async-done | bytes 524304 | tf_op jit(solution)/shard_map/reduce_scatter | solution.py:308
  (265 shorter events, 199.8 us)
Async XLA Ops:
  7.2 76.2 %all-gather.7.cloned.1.call-start = ((), (), s32[]{:S(2)}) async-start(), calls=%async_computation.6 | async-start | bytes 6488064 | tf_op jit(solution)/shard_map/all_gather | solution.py:93
  7.9 126.2 %all-gather.9.cloned.1.call-start = ((), (), s32[]{:S(2)}) async-start(), calls=%async_computation.7 | async-start | bytes 2621440 | tf_op jit(solution)/shard_map/all_gather | solution.py:126
  56.4 31.9 %copy-start.24 = (f32[1024]{0:T(1024)}, f32[1024]{0:T(1024)S(1)}, u32[]{:S(2)}) copy-start(f32[1024]{0:T(1024)S(1)} %convert_element_type.129) | copy-start | bytes 12292
  56.4 31.9 %copy-start.22 = (f32[1024]{0:T(1024)}, f32[1024]{0:T(1024)S(1)}, u32[]{:S(2)}) copy-start(f32[1024]{0:T(1024)S(1)} %convert_element_type.128) | copy-start | bytes 12292
  89.5 91.4 %all-gather.11.cloned.1.call-start = ((), (), s32[]{:S(2)}) async-start(), calls=%async_computation.8 | async-start | bytes 2621440 | tf_op jit(solution)/shard_map/all_gather | solution.py:125
  90.5 148.5 %all-gather.13.cloned.1.call-start = ((), (), s32[]{:S(2)}) async-start(), calls=%async_computation.9 | async-start | bytes 2162688 | tf_op jit(solution)/shard_map/all_gather | solution.py:95
  91.1 227.0 %all-gather.15.cloned.1.call-start = ((), (), s32[]{:S(2)}) async-start(), calls=%async_computation.10 | async-start | bytes 8650752 | tf_op jit(solution)/shard_map/all_gather | solution.py:99
  91.7 305.2 %all-gather.17.cloned.1.call-start = ((), (), s32[]{:S(2)}) async-start(), calls=%async_computation.11 | async-start | bytes 8650752 | tf_op jit(solution)/shard_map/all_gather | solution.py:101
  92.2 436.2 %reduce-scatter.9.cloned.1.call-start = ((), (), s32[]{:S(2)}) async-start(), calls=%async_computation.13 | async-start | bytes 2621440 | tf_op jit(solution)/shard_map/reduce_scatter | solution.py:258
  92.3 3.6 collective-permute-start
  95.9 4.6 collective-permute-start.1
  100.5 1.2 collective-permute-start.2
  101.8 3.7 collective-permute-start.3
  105.5 3.7 collective-permute-start.4
  485.8 88.2 %reduce-scatter.7.cloned.1.call-start = ((), (), s32[]{:S(2)}) async-start(), calls=%async_computation.12 | async-start | bytes 2621440 | tf_op jit(solution)/shard_map/reduce_scatter | solution.py:252
  488.5 236.4 %reduce-scatter.13.cloned.1.call-start = ((), (), s32[]{:S(2)}) async-start(), calls=%async_computation.15 | async-start | bytes 4325376 | tf_op jit(solution)/shard_map/reduce_scatter | solution.py:302
  492.2 81.7 %copy-start.23 = (f32[1024]{0:T(1024)S(1)}, f32[1024]{0:T(1024)}, u32[]{:S(2)}) copy-start(f32[1024]{0:T(1024)} %copy-done.22) | copy-start | bytes 12292
  492.2 81.7 %copy-start.25 = (f32[1024]{0:T(1024)S(1)}, f32[1024]{0:T(1024)}, u32[]{:S(2)}) copy-start(f32[1024]{0:T(1024)} %copy-done.24) | copy-start | bytes 12292
  492.2 81.8 %copy-start.27 = (f32[256]{0:T(256)S(1)}, f32[256]{0:T(256)}, u32[]{:S(2)}) copy-start(f32[256]{0:T(256)} %copy-done.26) | copy-start | bytes 3076
  492.3 81.7 %copy-start.29 = (f32[256]{0:T(256)S(1)}, f32[256]{0:T(256)}, u32[]{:S(2)}) copy-start(f32[256]{0:T(256)} %copy-done.28) | copy-start | bytes 3076
  492.3 392.5 %reduce-scatter.11.cloned.1.call-start = ((), (), s32[]{:S(2)}) async-start(), calls=%async_computation.14 | async-start | bytes 12976128 | tf_op jit(solution)/shard_map/reduce_scatter | solution.py:300
  493.7 88.0 %copy-start.12 = (bf16[256,16,64]{0,2,1:T(8,128)(2,1)}, bf16[256,16,64]{0,2,1:T(8,128)(2,1)S(1)}, u32[]{:S(2)}) copy-start(bf16[256,16,64]{0,2,1:T(8,128)(2,1)S(1)} %get-tuple-element.513) | copy-start | bytes 1572868
  581.7 669.3 %reduce-scatter.15.cloned.1.call-start = ((), (), s32[]{:S(2)}) async-start(), calls=%async_computation.16 | async-start | bytes 17301504 | tf_op jit(solution)/shard_map/reduce_scatter | solution.py:306
  592.8 1023.3 %reduce-scatter.17.cloned.1.call-start = ((), (), s32[]{:S(2)}) async-start(), calls=%async_computation.17 | async-start | bytes 17301504 | tf_op jit(solution)/shard_map/reduce_scatter | solution.py:308
  (38 other events, 225.3 us)
Sparse Core Ops, SparseCore 0:
  10.9 72.4 all-gather.6
  89.7 44.4 all-gather.8
  136.3 44.6 all-gather.10
  183.8 55.1 all-gather.12
  241.8 76.2 all-gather.14
  320.9 75.9 all-gather.16
  485.9 42.4 reduce-scatter.8
  530.8 43.1 reduce-scatter.6
  576.8 147.9 reduce-scatter.12
  731.3 153.4 reduce-scatter.10
  887.7 363.2 reduce-scatter.14
  1253.9 362.1 reduce-scatter.16
